TPU v7x, 32 devices: a whole 2x2x4 slice. The times are simulated.
32 devices in a mesh: src: 4 (over y, core), rcv: 8 (over z, x).
Axes of the slice: x: 2, y: 2, z: 4, core: 2. Of those that a mesh axis runs over, the one named last changes fastest.
Arguments:
- data: bfloat16 [2, 4096, 4096], P(None, ('src', 'rcv')), may hold values from -0.8984375 to 0.8984375
- fill_mask: int32 [4096, 4096], P(('src', 'rcv')), may hold values 0 or 1
- obliquity: float32 [4096], replicated, may hold values from 0.25 to 4
- aperture: int32 [8, 8, 8], P('src'), may hold values from 0 to 7, as said below
- lengths: int32 [8, 8], P('src', 'rcv'), may hold values from 1 to 8, as said below
Outputs:
- predicted: float32 [2, 4096, 4096], P(None, 'src', 'rcv')
Inputs may be any that keep to these rules, and one draw needn't show every extreme that they name: `aperture`: every entry is a tile index; the 8 entries of one output tile are distinct; only the first lengths entries of a list are used. `lengths`: some output tile uses all 8 entries of its list.
All inputs are finite; a program needn't handle non-finite values. No bound on the sum of `fill_mask` on one device may be relied on, other than what follows from the above.
Results may differ from a plain program's by a relative error of at most 0.0028.
Values may be sent and summed in bfloat16 or wider, within the bound.
No kernel may reach another device: no remote copies, remote signals or barrier semaphores. Data moves between devices by JAX's collectives and lax.ppermute only.
A program may use at most 128 MiB of HBM per device.

v0:
```python
import jax
import jax.numpy as jnp
from jax import lax
from jax.sharding import PartitionSpec as P

TILE_SIZE = 512


def complex_product(left_pair, right_pair):
    left_wide = jnp.concatenate([left_pair[0], left_pair[1]], axis=1)
    upper = jnp.concatenate([right_pair[0], right_pair[1]], axis=1)
    lower = jnp.concatenate([-right_pair[1], right_pair[0]], axis=1)
    right_wide = jnp.concatenate([upper, lower], axis=0)
    return jnp.dot(left_wide, right_wide, preferred_element_type=jnp.float32)


def predict_tile(tile_row, my_lists, slot_count, left_piece, column_data):

    def add_slot(slot_index, summed):
        inner_tile = my_lists[tile_row, slot_index]
        left_pair = left_piece(tile_row, slot_index, inner_tile)
        right_pair = lax.dynamic_slice(
            column_data, (0, inner_tile * TILE_SIZE, 0), (2, TILE_SIZE, TILE_SIZE)
        )
        return summed + complex_product(left_pair, right_pair)

    initial = jnp.zeros((TILE_SIZE, 2 * TILE_SIZE), jnp.float32)
    return -lax.fori_loop(0, slot_count, add_slot, initial)


def local(data, fill_mask, obliquity, aperture, lengths):
    local_rows = data.shape[1]
    station_total = data.shape[2]
    src_count = lax.axis_size("src")
    rcv_count = lax.axis_size("rcv")
    devices = src_count * rcv_count
    blocks = data.reshape(2, 1, local_rows, devices, local_rows)
    arrived = lax.all_to_all(blocks, ("src", "rcv"), split_axis=3, concat_axis=1, tiled=True)
    arrived = arrived.reshape(2, devices, local_rows, local_rows)
    transposed = jnp.transpose(arrived, (0, 3, 1, 2)).reshape(2, local_rows, station_total)
    filled = jnp.where(fill_mask[None] == 1, data, transposed)
    tile_block = lax.all_to_all(filled, "rcv", split_axis=2, concat_axis=1, tiled=True)
    span = tile_block.shape[1]
    gains = lax.dynamic_slice_in_dim(obliquity, lax.axis_index("src") * span, span)
    weighted = (tile_block.astype(jnp.float32) * gains[None, :, None]).astype(jnp.bfloat16)
    column_data = lax.all_gather(weighted, "src", axis=1, tiled=True)
    rcv_index = lax.axis_index("rcv")
    my_lists = lax.dynamic_index_in_dim(aperture, rcv_index, 1, keepdims=False)
    tile_rows = span // TILE_SIZE
    row_data = lax.all_gather(tile_block, "rcv", axis=2, tiled=True)

    def left_piece(tile_row, slot_index, inner_tile):
        return lax.dynamic_slice(
            row_data, (0, tile_row * TILE_SIZE, inner_tile * TILE_SIZE), (2, TILE_SIZE, TILE_SIZE)
        )

    results = []
    for tile_row in range(tile_rows):
        results.append(
            predict_tile(tile_row, my_lists, lengths[tile_row, 0], left_piece, column_data)
        )
    stacked = jnp.stack(results).reshape(tile_rows, TILE_SIZE, 2, TILE_SIZE)
    return jnp.transpose(stacked, (2, 0, 1, 3)).reshape(2, tile_rows * TILE_SIZE, TILE_SIZE)


def solution(mesh):
    placed = (
        P(None, ("src", "rcv"), None),
        P(("src", "rcv"), None),
        P(),
        P("src", None, None),
        P("src", "rcv"),
    )
    return jax.shard_map(
        local, mesh=mesh, in_specs=placed, out_specs=P(None, "src", "rcv"), check_vma=False
    )
```

profile of v0, /device:TPU:6, one launch (start us, length us, event | category | flops | bytes accessed | tf_op | source)
XLA Modules:
  0.0 575.6 jit_solution(8887815864550951217)
XLA Ops:
  6.5 3.1 copy.19
  11.1 6.1 %all-to-all-start = ((bf16[2,1,128,32,128]{2,4,0,1,3:T(8,128)(2,1)}), bf16[2,1,128,32,128]{2,4,0,1,3:T(8,128)(2,1)}, u32[]{:S(2)}, u32[]{:S(2)}) async-start(bf16[2,1,128,32,128]{2,4,0,1,3:T(8,128)(2,1)} %copy.17), calls=%async_computation | async-start | bytes 4194304 | tf_op jit(solution)/shard_map/all_to_all | solution.py:38
  17.3 1.9 broadcast_compare_fusion
  20.2 45.0 %all-to-all-done = bf16[2,1,128,32,128]{2,4,0,1,3:T(8,128)(2,1)} async-done(((bf16[2,1,128,32,128]{2,4,0,1,3:T(8,128)(2,1)}), bf16[2,1,128,32,128]{2,4,0,1,3:T(8,128)(2,1)}, u32[]{:S(2)}, u32[]{:S(2)}) %all-to-all-start) | async-done | bytes 2097184 | tf_op jit(solution)/shard_map/all_to_all | solution.py:38
  65.1 4.1 copy.18
  69.2 2.1 broadcast_select_fusion
  71.3 18.1 %copy.20 = bf16[2,128,4096]{1,0,2:T(2,128)(2,1)} copy(bf16[2,128,4096]{1,2,0:T(8,128)(2,1)S(1)} %broadcast_select_fusion) | data formatting | bytes 4194304 | tf_op jit(solution)/shard_map/jit(_where)/select_n | solution.py:41
  89.5 5.3 all-to-all-start.1
  94.8 48.2 %all-to-all-done.1 = bf16[2,128,4096]{1,0,2:T(2,128)(2,1)S(1)} async-done(((bf16[2,128,4096]{1,0,2:T(2,128)(2,1)}), bf16[2,128,4096]{1,0,2:T(2,128)(2,1)S(1)}, u32[]{:S(2)}, u32[]{:S(2)}) %all-to-all-start.1) | async-done | bytes 2097184 | tf_op jit(solution)/shard_map/all_to_all | solution.py:42
  144.3 4.7 copy.21
  149.1 2.1 multiply_convert_fusion
  152.6 55.1 %all-gather.5.cloned.1.call-done = bf16[2,4096,512]{2,1,0:T(8,128)(2,1)} async-done(((bf16[2,1024,512]{2,1,0:T(8,128)(2,1)}), bf16[2,4096,512]{2,1,0:T(8,128)(2,1)}) %all-gather.5.cloned.1.call-update) | async-done | bytes 8388624 | tf_op jit(solution)/shard_map/all_gather | solution.py:46
  207.7 230.3 %all-gather.3.cloned.1.call-done = bf16[2,1024,4096]{2,1,0:T(8,128)(2,1)} async-done(((bf16[2,1024,512]{2,1,0:T(8,128)(2,1)}), bf16[2,1024,4096]{2,1,0:T(8,128)(2,1)}) %all-gather.3.cloned.1.call-update) | async-done | bytes 16777232 | tf_op jit(solution)/shard_map/all_gather | solution.py:50
  438.2 58.5 %while.21 = (s32[]{:T(128)}, f32[512,1024]{1,0:T(8,128)S(1)}, s32[]{:T(128)}, s32[2,8]{1,0:T(2,128)S(1)}, bf16[2,1024,4096]{2,1,0:T(8,128)(2,1)}, /*index=5*/bf1...) while((s32[]{:T(128)}, f32[512,1024]{1,0:T(8,128)S(1)}, ...), condition=%wide.region_3.4_spmd, body=%wide.region_2.3_spmd.sunk | while | flops 1085538304 | bytes 11534561 | solution.py:28
  442.7 1.5 dynamic-slice_bitcast_fusion.13
  449.9 1.5 dynamic-slice_bitcast_fusion.13
  457.1 1.5 dynamic-slice_bitcast_fusion.13
  496.8 1.5 neg.13
  498.3 3.0 stack.10
  501.3 1.7 copy.23
  503.3 56.9 %while.20 = (s32[]{:T(128)}, f32[512,1024]{1,0:T(8,128)S(1)}, s32[]{:T(128)}, s32[2,8]{1,0:T(2,128)S(1)}, bf16[2,1024,4096]{2,1,0:T(8,128)(2,1)}, /*index=5*/bf1...) while((s32[]{:T(128)}, f32[512,1024]{1,0:T(8,128)S(1)}, ...), condition=%wide.region_1.2_spmd, body=%wide.region_0.1_spmd.sunk | while | flops 1085538304 | bytes 11534561 | solution.py:28
  560.2 1.5 neg.12
  561.7 3.0 stack.9
  566.3 2.5 pad_maximum_fusion
  (86 shorter events, 75.9 us)
Async XLA Ops:
  6.5 145.4 %copy-start = (s32[2,8,8]{2,1,0:T(8,128)S(1)}, s32[2,8,8]{2,1,0:T(8,128)}, u32[]{:S(2)}) copy-start(s32[2,8,8]{2,1,0:T(8,128)} %param.12) | copy-start | bytes 1540
  11.1 54.0 %all-to-all-start = ((bf16[2,1,128,32,128]{2,4,0,1,3:T(8,128)(2,1)}), bf16[2,1,128,32,128]{2,4,0,1,3:T(8,128)(2,1)}, u32[]{:S(2)}, u32[]{:S(2)}) async-start(bf16[2,1,128,32,128]{2,4,0,1,3:T(8,128)(2,1)} %copy.17), calls=%async_computation | async-start | bytes 4194304 | tf_op jit(solution)/shard_map/all_to_all | solution.py:38
  89.5 53.5 %all-to-all-start.1 = ((bf16[2,128,4096]{1,0,2:T(2,128)(2,1)}), bf16[2,128,4096]{1,0,2:T(2,128)(2,1)S(1)}, u32[]{:S(2)}, u32[]{:S(2)}) async-start(bf16[2,128,4096]{1,0,2:T(2,128)(2,1)} %copy.20), calls=%async_computation.1 | async-start | bytes 4194304 | tf_op jit(solution)/shard_map/all_to_all | solution.py:42
  94.8 112.9 %all-gather.5.cloned.1.call-start = ((), (), s32[]{:S(2)}) async-start(), calls=%async_computation.3 | async-start | bytes 10485760 | tf_op jit(solution)/shard_map/all_gather | solution.py:46
  143.0 1.3 copy-start.3
  144.3 4.7 dynamic-slice-start
  149.1 2.1 copy-start.2
  151.1 0.8 copy-start.5
  151.2 286.8 %all-gather.3.cloned.1.call-start = ((), (), s32[]{:S(2)}) async-start(), calls=%async_computation.2 | async-start | bytes 18874368 | tf_op jit(solution)/shard_map/all_gather | solution.py:50
  564.8 1.6 copy-start.4
  566.3 2.5 copy-start.1
Sparse Core Ops, SparseCore 0:
  151.3 56.3 all-gather.4
  209.7 228.1 all-gather.2
where the time goes:
time: 578 us; the launch traced here: 576 us
  waiting for transfers between devices  379 us (66%)
  local copies, waits for them, and re-layouts  67.9 us (12%)
  loops' own time  42.4 us (7%)
  other arithmetic  39.8 us (7%)
  matrix products  21.2 us (4%)
  between operations  13.6 us (2%)
  starting transfers between devices  11.5 us (2%)
    all_gather x1, waiting for transfers between devices, local(): row_data = lax.all_gather(tile_block, 'rcv', axis=2, tiled=True)  230 us
    all_gather x1, waiting for transfers between devices, local(): column_data = lax.all_gather(weighted, 'src', axis=1, tiled=True)  55.1 us
    all_to_all x1, waiting for transfers between devices, local(): lax.all_to_all(filled, 'rcv', split_axis=2, concat_axis=1, tiled=True)  48.2 us
    all_to_all x1, waiting for transfers between devices, local(): lax.all_to_all(blocks, ('src', 'rcv'), split_axis=3, concat_axis=1, tiled...  45 us
    another operation x2, loops' own time, predict_tile(): return -lax.fori_loop(0, slot_count, add_slot, initial)  42.4 us
    squeeze x16, local copies, waits for them, and re-layouts, complex_product(): left_wide = jnp.concatenate([left_pair[0], left_pair[1]], axis=1)  23.7 us
    dot_general x16, matrix products, complex_product(): return jnp.dot(left_wide, right_wide, preferred_element_type=jnp.float32)  21.2 us
    neg x16, other arithmetic, complex_product(): lower = jnp.concatenate([-right_pair[1], right_pair[0]], axis=1)  18.7 us
  transfers between devices with their start and end apart: 4, of which 4 were waited for; matrix products, arithmetic and copies ran while one was open for 1% of the time, Pallas kernels for 0%

commit v1 on v0

--- a/solution.py
+++ b/solution.py
@@ -43,7 +43,12 @@
     span = tile_block.shape[1]
     gains = lax.dynamic_slice_in_dim(obliquity, lax.axis_index("src") * span, span)
     weighted = (tile_block.astype(jnp.float32) * gains[None, :, None]).astype(jnp.bfloat16)
-    column_data = lax.all_gather(weighted, "src", axis=1, tiled=True)
+    ring = [weighted]
+    for hop in range(3):
+        ring.append(lax.ppermute(ring[-1], "src", [(dev, (dev + 1) % 4) for dev in range(4)]))
+    column_data = jnp.roll(
+        jnp.concatenate(ring[::-1], axis=1), (lax.axis_index("src") + 1) * ring[0].shape[1], axis=1
+    )
     rcv_index = lax.axis_index("rcv")
     my_lists = lax.dynamic_index_in_dim(aperture, rcv_index, 1, keepdims=False)
     tile_rows = span // TILE_SIZE

time: 578 us -> 513 us (0.89)
  waiting for transfers between devices: 379 us -> 241 us
  blocking collectives: 0 us -> 53 us
  local copies, waits for them, and re-layouts: 67.9 us -> 94.7 us
    all_gather x1, waiting for transfers between devices: 230 us -> 120 us  [local(): row_data = lax.all_gather(tile_block, 'rcv', axis=2, tiled=True)]
    ppermute x0 -> x3, waiting for transfers between devices: none -> 76.1 us  [local(): lax.ppermute(ring[-1], 'src', [(dev, (dev + 1) % 4) for dev in range(4)])]
    all_gather x1 -> x0, waiting for transfers between devices: 55.1 us -> none  [local(): column_data = lax.all_gather(weighted, 'src', axis=1, tiled=True)]
    all_to_all x0 -> x1, blocking collectives: none -> 53 us  [local(): lax.all_to_all(filled, 'rcv', split_axis=2, concat_axis=1, tiled=True)]
    all_to_all x1 -> x0, waiting for transfers between devices: 48.2 us -> none  [local(): lax.all_to_all(filled, 'rcv', split_axis=2, concat_axis=1, tiled=True)]
    unnamed x13 -> x22, local copies, waits for them, and re-layouts: 5.65 us -> 24.1 us
    dynamic_slice x0 -> x1, local copies, waits for them, and re-layouts: none -> 7.32 us  [local(): jnp.roll(jnp.concatenate(ring[::-1], axis=1), (lax.axis_index('src') + 1)...]
  transfers between devices with their start and end apart: 4 -> 5, of which waited for: 4 -> 5; matrix products, arithmetic and copies ran while one was open for 1% -> 6% of each run, Pallas kernels for 0% -> 0%
where the time goes in v1:
time: 513 us; the launch traced here: 511 us
  waiting for transfers between devices  241 us (47%)
  local copies, waits for them, and re-layouts  94.7 us (18%)
  blocking collectives  53 us (10%)
  loops' own time  43.3 us (8%)
  other arithmetic  38 us (7%)
  matrix products  21.3 us (4%)
  between operations  13.6 us (3%)
  starting transfers between devices  6.17 us (1%)
    all_gather x1, waiting for transfers between devices, local(): row_data = lax.all_gather(tile_block, 'rcv', axis=2, tiled=True)  120 us
    ppermute x3, waiting for transfers between devices, local(): lax.ppermute(ring[-1], 'src', [(dev, (dev + 1) % 4) for dev in range(4)])  76.1 us
    all_to_all x1, blocking collectives, local(): lax.all_to_all(filled, 'rcv', split_axis=2, concat_axis=1, tiled=True)  53 us
    all_to_all x1, waiting for transfers between devices, local(): lax.all_to_all(blocks, ('src', 'rcv'), split_axis=3, concat_axis=1, tiled...  44.9 us
    another operation x2, loops' own time, predict_tile(): return -lax.fori_loop(0, slot_count, add_slot, initial)  43.3 us
    unnamed x22, local copies, waits for them, and re-layouts  24.1 us
    squeeze x16, local copies, waits for them, and re-layouts, complex_product(): left_wide = jnp.concatenate([left_pair[0], left_pair[1]], axis=1)  23.6 us
    dot_general x16, matrix products, complex_product(): return jnp.dot(left_wide, right_wide, preferred_element_type=jnp.float32)  21.3 us
  transfers between devices with their start and end apart: 5, of which 5 were waited for; matrix products, arithmetic and copies ran while one was open for 6% of the time, Pallas kernels for 0%

profile of v1, /device:TPU:6, one launch (start us, length us, event | category | flops | bytes accessed | tf_op | source)
XLA Modules:
  0.0 510.9 jit_solution(4813332350383859077)
XLA Ops:
  6.5 3.1 copy.19
  11.1 6.1 %all-to-all-start = ((bf16[2,1,128,32,128]{2,4,0,1,3:T(8,128)(2,1)}), bf16[2,1,128,32,128]{2,4,0,1,3:T(8,128)(2,1)}, u32[]{:S(2)}, u32[]{:S(2)}) async-start(bf16[2,1,128,32,128]{2,4,0,1,3:T(8,128)(2,1)} %copy.17), calls=%async_computation | async-start | bytes 4194304 | tf_op jit(solution)/shard_map/all_to_all | solution.py:38
  17.3 1.9 broadcast_compare_fusion
  20.2 44.9 %all-to-all-done = bf16[2,1,128,32,128]{2,4,0,1,3:T(8,128)(2,1)} async-done(((bf16[2,1,128,32,128]{2,4,0,1,3:T(8,128)(2,1)}), bf16[2,1,128,32,128]{2,4,0,1,3:T(8,128)(2,1)}, u32[]{:S(2)}, u32[]{:S(2)}) %all-to-all-start) | async-done | bytes 2097184 | tf_op jit(solution)/shard_map/all_to_all | solution.py:38
  65.1 4.1 copy.18
  69.2 2.1 broadcast_select_fusion
  71.3 17.8 %copy.20 = bf16[2,128,4096]{1,0,2:T(2,128)(2,1)S(1)} copy(bf16[2,128,4096]{1,2,0:T(8,128)(2,1)S(1)} %broadcast_select_fusion) | data formatting | bytes 4194304 | tf_op jit(solution)/shard_map/jit(_where)/select_n | solution.py:41
  89.2 53.0 %all_to_all.33 = bf16[2,128,4096]{1,0,2:T(2,128)(2,1)S(1)} all-to-all(bf16[2,128,4096]{1,0,2:T(2,128)(2,1)S(1)} %copy.20), channel_id=1, replica_groups=mesh['src'=4,'rcv'=8] {'rcv'}, dimensions={2} | all-to-all | bytes 4194304 | tf_op jit(solution)/shard_map/all_to_all | solution.py:42
  142.2 3.8 copy.21
  149.3 25.5 %collective-permute-done = bf16[2,1024,512]{2,1,0:T(8,128)(2,1)S(1)} collective-permute-done((bf16[2,1024,512]{2,1,0:T(8,128)(2,1)S(1)}, bf16[2,1024,512]{2,1,0:T(8,128)(2,1)S(1)}, u32[]{:S(2)}, u32[]{:S(2)}) %collective-permute-start) | collective-permute-done | bytes 2097184 | tf_op jit(solution)/shard_map/ppermute | solution.py:48
  174.8 25.6 %collective-permute-done.1 = bf16[2,1024,512]{2,1,0:T(8,128)(2,1)} collective-permute-done((bf16[2,1024,512]{2,1,0:T(8,128)(2,1)S(1)}, bf16[2,1024,512]{2,1,0:T(8,128)(2,1)}, u32[]{:S(2)}, u32[]{:S(2)}) %collective-permute-start.1) | collective-permute-done | bytes 2097184 | tf_op jit(solution)/shard_map/ppermute | solution.py:48
  201.0 25.1 %collective-permute-done.2 = bf16[2,1024,512]{2,1,0:T(8,128)(2,1)} collective-permute-done((bf16[2,1024,512]{2,1,0:T(8,128)(2,1)}, bf16[2,1024,512]{2,1,0:T(8,128)(2,1)}, u32[]{:S(2)}, u32[]{:S(2)}) %collective-permute-start.2) | collective-permute-done | bytes 2097184 | tf_op jit(solution)/shard_map/ppermute | solution.py:48
  226.1 3.1 constant_dynamic-update-slice_fusion.7
  229.2 3.0 constant_dynamic-update-slice_fusion.6
  236.1 3.2 constant_dynamic-update-slice_fusion.3
  239.3 3.1 constant_dynamic-update-slice_fusion.2
  245.3 7.3 %constant_dynamic-slice_fusion.2 = bf16[2,4096,512]{2,1,0:T(8,128)(2,1)} fusion(bf16[2,8192,512]{2,1,0:T(8,128)(2,1)} %constant_dynamic-update-slice_fusion, s32[]{:T(128)S(6)} %select_n.42), kind=kLoop, calls=%fused_computation.48 | loop fusion | bytes 16777220 | tf_op jit(solution)/shard_map/jit(_roll_dynamic)/dynamic_slice | solution.py:49
  252.6 119.8 %all-gather.2.cloned.1.call-done = bf16[2,1024,4096]{2,1,0:T(8,128)(2,1)} async-done(((bf16[2,1024,512]{2,1,0:T(8,128)(2,1)}), bf16[2,1024,4096]{2,1,0:T(8,128)(2,1)}) %all-gather.2.cloned.1.call-update) | async-done | bytes 16777232 | tf_op jit(solution)/shard_map/all_gather | solution.py:55
  372.7 57.9 %while.20 = (s32[]{:T(128)}, f32[512,1024]{1,0:T(8,128)S(1)}, s32[]{:T(128)}, s32[2,8]{1,0:T(2,128)S(1)}, bf16[2,1024,4096]{2,1,0:T(8,128)(2,1)}, /*index=5*/bf1...) while((s32[]{:T(128)}, f32[512,1024]{1,0:T(8,128)S(1)}, ...), condition=%wide.region_1.2_spmd, body=%wide.region_0.1_spmd.sunk | while | flops 1085538304 | bytes 11534553 | solution.py:28
  432.1 3.0 stack.9
  435.1 1.7 copy.22
  437.1 58.4 %while.21 = (s32[]{:T(128)}, f32[512,1024]{1,0:T(8,128)S(1)}, s32[]{:T(128)}, s32[2,8]{1,0:T(2,128)S(1)}, bf16[2,1024,4096]{2,1,0:T(8,128)(2,1)}, /*index=5*/bf1...) while((s32[]{:T(128)}, f32[512,1024]{1,0:T(8,128)S(1)}, ...), condition=%wide.region_3.4_spmd, body=%wide.region_2.3_spmd.sunk | while | flops 1085538304 | bytes 11534553 | solution.py:28
  496.9 3.0 stack.10
  501.6 2.5 pad_maximum_fusion
  (98 shorter events, 91.3 us)
Async XLA Ops:
  6.5 193.8 %copy-start = (s32[2,8,8]{2,1,0:T(8,128)S(1)}, s32[2,8,8]{2,1,0:T(8,128)}, u32[]{:S(2)}) copy-start(s32[2,8,8]{2,1,0:T(8,128)} %param.12) | copy-start | bytes 1540
  11.1 54.0 %all-to-all-start = ((bf16[2,1,128,32,128]{2,4,0,1,3:T(8,128)(2,1)}), bf16[2,1,128,32,128]{2,4,0,1,3:T(8,128)(2,1)}, u32[]{:S(2)}, u32[]{:S(2)}) async-start(bf16[2,1,128,32,128]{2,4,0,1,3:T(8,128)(2,1)} %copy.17), calls=%async_computation | async-start | bytes 4194304 | tf_op jit(solution)/shard_map/all_to_all | solution.py:38
  17.3 355.2 %all-gather.2.cloned.1.call-start = ((), (), s32[]{:S(2)}) async-start(), calls=%async_computation.2 | async-start | bytes 18874368 | tf_op jit(solution)/shard_map/all_gather | solution.py:55
  145.9 1.6 copy-start.2
  147.5 52.8 %copy-start.6 = (s32[2,1]{0,1:T(1,128)S(1)}, s32[2,1]{0,1:T(1,128)}, u32[]{:S(2)}) copy-start(s32[2,1]{0,1:T(1,128)} %param.13) | copy-start | bytes 28
  148.0 1.3 copy-start.3
  149.3 25.5 %collective-permute-start = (bf16[2,1024,512]{2,1,0:T(8,128)(2,1)S(1)}, bf16[2,1024,512]{2,1,0:T(8,128)(2,1)S(1)}, u32[]{:S(2)}, u32[]{:S(2)}) collective-permute-start(bf16[2,1024,512]{2,1,0:T(8,128)(2,1)S(1)} %multiply_convert_fusion), channel_id=1, source_target_pairs={{0,8},{8,16},{16,24},{24,0},{1,9},{9,17},{17,25},{25,1},{2,10},{10... | collective-permute-start | bytes 6291464 | tf_op jit(solution)/shard_map/ppermute | solution.py:48
  174.8 25.6 %collective-permute-start.1 = (bf16[2,1024,512]{2,1,0:T(8,128)(2,1)S(1)}, bf16[2,1024,512]{2,1,0:T(8,128)(2,1)}, u32[]{:S(2)}, u32[]{:S(2)}) collective-permute-start(bf16[2,1024,512]{2,1,0:T(8,128)(2,1)S(1)} %collective-permute-done), channel_id=1, source_target_pairs={{0,8},{8,16},{16,24},{24,0},{1,9},{9,17},{17,25},{25,1},{2,10},{10... | collective-permute-start | bytes 6291464 | tf_op jit(solution)/shard_map/ppermute | solution.py:48
  200.3 25.8 %collective-permute-start.2 = (bf16[2,1024,512]{2,1,0:T(8,128)(2,1)}, bf16[2,1024,512]{2,1,0:T(8,128)(2,1)}, u32[]{:S(2)}, u32[]{:S(2)}) collective-permute-start(bf16[2,1024,512]{2,1,0:T(8,128)(2,1)} %collective-permute-done.1), channel_id=1, source_target_pairs={{0,8},{8,16},{16,24},{24,0},{1,9},{9,17},{17,25},{25,1},{2,10},{10... | collective-permute-start | bytes 6291464 | tf_op jit(solution)/shard_map/ppermute | solution.py:48
  232.2 2.4 copy-start.4
  500.0 1.6 copy-start.5
  501.6 2.5 copy-start.1
Sparse Core Ops, SparseCore 0:
  146.1 226.3 all-gather.1
